TPU v7x, 512 devices: a whole 4x8x8 slice. The times are simulated.
512 devices in a mesh: fsdp: 64 (over z, x, y_lo), tp: 8 (over y_hi, core).
Axes of the slice: x: 4, y: 8 (y_hi: 4, y_lo: 2; y = y_hi * 2 + y_lo), z: 8, core: 2. Of those that a mesh axis runs over, the one named last changes fastest.
Arguments:
- gate_pre: bfloat16 [8192, 14336], P('fsdp', 'tp'), may hold values from -6 to 6
- up_pre: bfloat16 [8192, 14336], P('fsdp', 'tp'), may hold values from -6 to 6
- down_weight: bfloat16 [14336, 4096], P('tp', 'fsdp'), may hold values from -0.046875 to 0.046875
Outputs:
- mixed: bfloat16 [8192, 4096], P('fsdp', 'tp')
All inputs are finite; a program needn't handle non-finite values.
Results may differ from a plain program's by a relative error of at most 0.0049.
Values may be sent and summed in bfloat16 or wider, within the bound.
A program may use at most 64 MiB of HBM per device.

v0:
```python
import jax
import jax.numpy as jnp
from jax import lax
from jax.sharding import PartitionSpec as P


def shards(gate_pre, up_pre, down_weight):
    hidden = (jax.nn.silu(gate_pre.astype(jnp.float32)) * up_pre.astype(jnp.float32)).astype(
        jnp.bfloat16
    )
    terms = jnp.dot(
        hidden,
        lax.all_gather(down_weight, "fsdp", axis=1, tiled=True),
        preferred_element_type=jnp.float32,
    )
    totals = lax.psum(terms, "tp")
    share = totals.shape[1] // lax.axis_size("tp")
    result = lax.dynamic_slice_in_dim(totals, lax.axis_index("tp") * share, share, 1)
    return result.astype(jnp.bfloat16)


def solution(mesh):
    return jax.shard_map(
        shards,
        mesh=mesh,
        in_specs=(P("fsdp", "tp"), P("fsdp", "tp"), P("tp", "fsdp")),
        out_specs=P("fsdp", "tp"),
        check_vma=False,
    )
```

profile of v0, /device:TPU:1, one launch (start us, length us, event | category | flops | bytes accessed | tf_op | source)
XLA Modules:
  0.0 456.0 jit_solution(7326851797001008196)
XLA Ops:
  6.5 0.0 all-gather.2.cloned.1.call-start
  6.5 0.7 all-gather.2.cloned.1.call-update
  7.3 331.1 %all-gather.2.cloned.1.call-done = bf16[1792,4096]{0,1:T(8,128)(2,1)} async-done(((bf16[1792,64]{0,1:T(8,128)(2,1)}), bf16[1792,4096]{0,1:T(8,128)(2,1)}) %all-gather.2.cloned.1.call-update) | async-done | bytes 14680080 | tf_op jit(solution)/shard_map/all_gather | solution.py:13
  338.4 10.2 %fusion.5 = f32[128,4096]{1,0:T(8,128)S(1)} fusion(bf16[1792,4096]{0,1:T(8,128)(2,1)} %all-gather.2.cloned.1.call-done, bf16[128,1792]{1,0:T(8,128)(2,1)} %param.4, bf16[128,1792]{1,0:T(8,128)(2,1)} %param.3), kind=kOutput, calls=%fused_computation.7 | convolution fusion | flops 1880883200 | bytes 17694720 | tf_op jit(solution)/shard_map/dot_general | solution.py:11
  348.7 99.8 %all-reduce.1 = bf16[128,4096]{1,0:T(8,128)(2,1)S(1)} all-reduce(f32[128,4096]{1,0:T(8,128)S(1)} %fusion.5), channel_id=1, replica_groups=mesh['fsdp'=64,'tp'=8] {'tp'}, use_global_device_ids=true, to_apply=%region_0.1 | all-reduce | flops 524288 | bytes 3145728 | tf_op jit(solution)/shard_map/psum | solution.py:16
  448.5 0.7 dynamic-slice_convert_fusion
Async XLA Ops:
  6.5 331.9 %all-gather.2.cloned.1.call-start = ((), (), s32[]{:S(2)}) async-start(), calls=%async_computation | async-start | bytes 14909440 | tf_op jit(solution)/shard_map/all_gather | solution.py:13
Sparse Core Ops, SparseCore 0:
  9.4 328.9 all-gather.1
where the time goes:
time: 456 us
  waiting for transfers between devices  332 us (73%)
  blocking collectives  99.8 us (22%)
  between operations  13.4 us (3%)
  matrix products  10.2 us (2%)
    all_gather x1, waiting for transfers between devices, shards(): lax.all_gather(down_weight, 'fsdp', axis=1, tiled=True)  331 us
    psum x1, blocking collectives, shards(): totals = lax.psum(terms, 'tp')  99.8 us
    dot_general x1, matrix products, shards(): jnp.dot(hidden, lax.all_gather(down_weight, 'fsdp', axis=1, tiled=True),...  10.2 us
  transfers between devices with their start and end apart: 1, of which 1 were waited for; matrix products, arithmetic and copies ran while one was open for 0% of the time, Pallas kernels for 0%

commit v1 on v0

v1 whole, which is shorter than its diff:
```python
import jax
import jax.numpy as jnp
from jax import lax
from jax.experimental import pallas as pl
from jax.experimental.pallas import tpu as pltpu
from jax.sharding import PartitionSpec as P

MESH = pl.DeviceIdType.MESH
X, Y, Z = 4, 8, 8
ROWS, COLS, HALF = 128, 64, 896
STEPS = 4


def kernel(
    gate_hbm, up_hbm, w_hbm, out_ref,
    gate, up, h_send, a_all, b_all, part, other, out_buf, s_buf, r_buf, x_buf,
    load_sem, wx_sem, ax_sem, x_sem, xf_sem, z_sem, c_sem, y_sem, f_sem,
):
    f, t = lax.axis_index("fsdp"), lax.axis_index("tp")
    x, q, z = (f // 2) % X, f % 2, f // (2 * X)
    y, c = (t // 2) * 2 + q, t % 2
    p = 1 - q

    def at(x, y, z, c):
        return (z * 2 * X + x * 2 + y % 2, (y // 2) * 2 + c)

    right, left = at((x + 1) % X, y, z, c), at((x + 3) % X, y, z, c)
    across = at((x + 2) % X, y, z, c)
    north, south = at(x, (y + 1) % Y, z, c), at(x, (y + 7) % Y, z, c)
    ahead, behind = at(x, y, (z + 1) % Z, c), at(x, y, (z + 7) % Z, c)
    twin = at(x, y, z, 1 - c)
    mate = at(x, y + 1 - 2 * q, z, c)

    def send(src, dst, sems, device):
        copy = pltpu.make_async_remote_copy(
            src_ref=src, dst_ref=dst, send_sem=sems.at[0], recv_sem=sems.at[1],
            device_id=device, device_id_type=MESH,
        )
        copy.start()
        return copy

    mine = pl.ds(pl.multiple_of(q * HALF, 128), HALF)
    theirs = pl.ds(pl.multiple_of(p * HALF, 128), HALF)

    def a_at(x, q, start=0, size=ROWS):
        return a_all.at[q, pl.ds(pl.multiple_of(x * ROWS + start, 16), size)]

    def b_at(z, q, start=0, size=COLS):
        return b_all.at[pl.ds(pl.multiple_of((z * 2 + q) * COLS + start, 16), size)]

    loads = [
        pltpu.make_async_copy(w_hbm.at[:, mine], b_at(z, q), load_sem.at[0]),
        pltpu.make_async_copy(gate_hbm.at[:, theirs], gate.at[1], load_sem.at[1]),
        pltpu.make_async_copy(up_hbm.at[:, theirs], up.at[1], load_sem.at[2]),
        pltpu.make_async_copy(gate_hbm.at[:, mine], gate.at[0], load_sem.at[3]),
        pltpu.make_async_copy(up_hbm.at[:, mine], up.at[0], load_sem.at[4]),
    ]
    for load in loads:
        load.start()

    barrier = pltpu.get_barrier_semaphore()
    for peer in (right, left, across, north, south, ahead, behind, twin):
        pl.semaphore_signal(barrier, inc=1, device_id=peer, device_id_type=MESH)
    pl.semaphore_wait(barrier, 8)

    copies = []

    w_swap = send(w_hbm.at[:, theirs], b_at(z, q), wx_sem, mate)

    def z_hop(step, piece):
        who = q if piece == 0 else p
        cut = COLS if step < STEPS - 1 else COLS // 2
        fwd, back = (z + Z - step) % Z, (z + step) % Z
        up_src = b_at(fwd, who, 0, cut)
        down_src = b_at(back, who, COLS - cut, cut)
        return (
            send(up_src, up_src, z_sem.at[0, step, piece], ahead),
            send(down_src, down_src, z_sem.at[1, step, piece], behind),
        )

    def x_hop(piece):
        src = a_at(x, q if piece == 0 else p)
        return send(src, src, x_sem.at[0, piece], right), send(src, src, x_sem.at[1, piece], left)

    def x_forward(piece):
        who = q if piece == 0 else p
        fwd = a_at((x + 3) % X, who, 0, ROWS // 2)
        back = a_at((x + 1) % X, who, ROWS // 2, ROWS // 2)
        return send(fwd, fwd, xf_sem.at[0, piece], right), send(back, back, xf_sem.at[1, piece], left)

    def landed(pair):
        for copy in pair:
            copy.wait_recv()

    loads[0].wait()
    z0a = z_hop(0, 0)

    def act(i):
        g = gate[i].astype(jnp.float32)
        return (g / (1.0 + jnp.exp(-g)) * up[i].astype(jnp.float32)).astype(jnp.bfloat16)

    loads[1].wait()
    loads[2].wait()
    h_send[...] = act(1)
    a_swap = send(h_send, a_at(x, q), ax_sem, mate)
    loads[3].wait()
    loads[4].wait()
    a_at(x, q)[...] = act(0)
    x0a = x_hop(0)
    w_swap.wait_recv()
    z0b = z_hop(0, 1)
    landed(z0a)
    z1a = z_hop(1, 0)
    landed(z0b)
    z1b = z_hop(1, 1)
    a_swap.wait_recv()
    x0b = x_hop(1)
    landed(z1a)
    z2a = z_hop(2, 0)
    landed(x0a)
    x1a = x_forward(0)
    landed(z1b)
    z2b = z_hop(2, 1)
    landed(z2a)
    z3a = z_hop(3, 0)
    landed(x0b)
    x1b = x_forward(1)
    landed(z2b)
    z3b = z_hop(3, 1)
    for pair in (x1a, x1b, z3a, z3b):
        landed(pair)
    for pair in (z0a, z0b, z1a, z1b, z2a, z2b, z3a, z3b, x0a, x0b, x1a, x1b):
        for copy in pair:
            copy.wait_send()
    w_swap.wait_send()
    a_swap.wait_send()

    def target(i):
        odd = i % 2
        return (y + 4 + (1 - odd) * (i // 2) - odd * ((i + 1) // 2)) % Y

    def core_copy(to):
        return pltpu.make_async_remote_copy(
            src_ref=part.at[1 - c, to], dst_ref=other.at[to],
            send_sem=c_sem.at[0, to], recv_sem=c_sem.at[1, to],
            device_id=twin, device_id_type=MESH,
        )

    def product(i, carry):
        to = target(i)
        b = b_all[pl.ds(pl.multiple_of((to // 2) * 256, 256), 256)]
        r = lax.dot_general(
            a_all[to % 2], b, (((1,), (1,)), ((), ())), preferred_element_type=jnp.float32
        )
        part[0, to] = r[:, :128]
        part[1, to] = r[:, 128:]
        core_copy(to).start()
        return carry

    lax.fori_loop(0, Y, product, 0)

    def own(to, start=0, size=4 * ROWS):
        rows = pl.ds(start, size)
        return part[c, to, rows] + other[to, rows]

    half = 2 * ROWS
    far = (y + 4) % Y
    core_copy(far).wait_recv()
    s_buf[0, 0, :half] = own(far, 0, half).astype(jnp.bfloat16)
    s_buf[1, 0, half:] = own(far, half, half).astype(jnp.bfloat16)

    def y_hop(way, step):
        rows = pl.ds(way * half, half) if step == 0 else pl.ds(0, 2 * half)
        return send(
            s_buf.at[way, step, rows], r_buf.at[way, step, rows],
            y_sem.at[way, step], north if way == 0 else south,
        )

    hops = [y_hop(0, 0), y_hop(1, 0)]
    for step in range(1, STEPS):
        for way in range(2):
            to = (y + (STEPS - step if way == 0 else Y - STEPS + step)) % Y
            core_copy(to).wait_recv()
            came = hops[2 * (step - 1) + way]
            came.wait_recv()
            if step == 1:
                with_half, without = (0, half) if way == 0 else (half, 0)
                s_buf[way, step, with_half : with_half + half] = (
                    own(to, with_half, half)
                    + r_buf[way, 0, with_half : with_half + half].astype(jnp.float32)
                ).astype(jnp.bfloat16)
                s_buf[way, step, without : without + half] = own(to, without, half).astype(jnp.bfloat16)
            else:
                s_buf[way, step] = (own(to) + r_buf[way, step - 1].astype(jnp.float32)).astype(jnp.bfloat16)
            hops.append(y_hop(way, step))
    core_copy(y).wait_recv()
    hops[-2].wait_recv()
    hops[-1].wait_recv()
    total = own(y) + r_buf[0, STEPS - 1].astype(jnp.float32) + r_buf[1, STEPS - 1].astype(jnp.float32)
    x_buf[...] = total.astype(jnp.bfloat16).reshape(X, ROWS, 128)

    outs = []
    for i, device in ((1, right), (3, left), (2, across)):
        outs.append(send(x_buf.at[(x + i) % X], out_buf.at[x], f_sem.at[i], device))
    keep = pltpu.make_async_copy(x_buf.at[x], out_buf.at[x], load_sem.at[0])
    keep.start()
    keep.wait()
    for copy in outs:
        copy.wait_recv()
    for i in range(X):
        out_ref[:, i * 128 : (i + 1) * 128] = out_buf[i]
    for copy in outs + hops:
        copy.wait_send()

    def drain(i, carry):
        core_copy(i).wait_send()
        return carry

    lax.fori_loop(0, Y, drain, 0)


def shards(gate_pre, up_pre, down_weight):
    dma = pltpu.SemaphoreType.DMA
    bf16, f32 = jnp.bfloat16, jnp.float32
    return pl.pallas_call(
        kernel,
        out_shape=jax.ShapeDtypeStruct((ROWS, 512), bf16),
        in_specs=[pl.BlockSpec(memory_space=pl.ANY)] * 3,
        out_specs=pl.BlockSpec(memory_space=pltpu.VMEM),
        scratch_shapes=[
            pltpu.VMEM((2, ROWS, HALF), bf16),
            pltpu.VMEM((2, ROWS, HALF), bf16),
            pltpu.VMEM((ROWS, HALF), bf16),
            pltpu.VMEM((2, X * ROWS, HALF), bf16),
            pltpu.VMEM((Z * 2 * COLS, HALF), bf16),
            pltpu.VMEM((2, Y, X * ROWS, 128), f32),
            pltpu.VMEM((Y, X * ROWS, 128), f32),
            pltpu.VMEM((X, ROWS, 128), bf16),
            pltpu.VMEM((2, STEPS, X * ROWS, 128), bf16),
            pltpu.VMEM((2, STEPS, X * ROWS, 128), bf16),
            pltpu.VMEM((X, ROWS, 128), bf16),
            dma((5,)),
            dma((2,)),
            dma((2,)),
            dma((2, 2, 2)),
            dma((2, 2, 2)),
            dma((2, STEPS, 2, 2)),
            dma((2, Y)),
            dma((2, STEPS, 2)),
            dma((X, 2)),
        ],
        compiler_params=pltpu.CompilerParams(
            collective_id=0, has_side_effects=True, vmem_limit_bytes=48 << 20
        ),
        name="down_projection",
    )(gate_pre, up_pre, down_weight.T)


def solution(mesh):
    return jax.shard_map(
        shards,
        mesh=mesh,
        in_specs=(P("fsdp", "tp"), P("fsdp", "tp"), P("tp", "fsdp")),
        out_specs=P("fsdp", "tp"),
        check_vma=False,
    )
```

time: 456 us -> 68.2 us (0.15)
  the two profiles are of different devices: /device:TPU:1 before, /device:TPU:8 now
where the time goes in v1:
time: 68.2 us; the launch traced here: 68 us
  Pallas kernels  64.3 us (94%)
  local copies, waits for them, and re-layouts  3.63 us (5%)
    pallas_call x1, Pallas kernels, shards(): pl.pallas_call(kernel, out_shape=jax.ShapeDtypeStruct((ROWS, 512), bf16),...  64.3 us
    unnamed x7, local copies, waits for them, and re-layouts  3.63 us

profile of v1, /device:TPU:8, one launch (start us, length us, event | category | flops | bytes accessed | tf_op | source)
XLA Modules:
  0.0 68.0 jit_solution(13687171166907836570)
XLA Ops:
  0.0 0.0 copy-start
  0.0 1.0 %copy-done = bf16[128,1792]{1,0:T(8,128)(2,1)S(1)} copy-done((bf16[128,1792]{1,0:T(8,128)(2,1)S(1)}, bf16[128,1792]{1,0:T(8,128)(2,1)}, u32[]{:S(2)}) %copy-start) | copy-done | bytes 458776
  1.0 0.0 copy-start.1
  1.0 1.0 %copy-done.1 = bf16[128,1792]{1,0:T(8,128)(2,1)S(1)} copy-done((bf16[128,1792]{1,0:T(8,128)(2,1)S(1)}, bf16[128,1792]{1,0:T(8,128)(2,1)}, u32[]{:S(2)}) %copy-start.1) | copy-done | bytes 458776
  2.0 0.0 copy-start.2
  2.0 0.9 %copy-done.2 = bf16[1792,64]{0,1:T(8,128)(2,1)S(1)} copy-done((bf16[1792,64]{0,1:T(8,128)(2,1)S(1)}, bf16[1792,64]{0,1:T(8,128)(2,1)}, u32[]{:S(2)}) %copy-start.2) | copy-done | bytes 229400
  3.0 64.3 %down_projection.1 = bf16[128,512]{1,0:T(8,128)(2,1)S(1)} custom-call(bf16[128,1792]{1,0:T(8,128)(2,1)S(1)} %copy-done, bf16[128,1792]{1,0:T(8,128)(2,1)S(1)} %copy-done.1, bf16[64,1792]{1,0:T(8,128)(2,1)S(1)} %bitcast.1), custom_call_target="tpu_custom_call" | custom-call | tf_op jit(solution)/shard_map/down_projection/pallas_call | solution.py:225
  67.3 0.7 copy.5
Async XLA Ops:
  0.0 1.0 %copy-start = (bf16[128,1792]{1,0:T(8,128)(2,1)S(1)}, bf16[128,1792]{1,0:T(8,128)(2,1)}, u32[]{:S(2)}) copy-start(bf16[128,1792]{1,0:T(8,128)(2,1)} %gate_hbm.1) | copy-start | bytes 1376260
  1.0 1.0 %copy-start.1 = (bf16[128,1792]{1,0:T(8,128)(2,1)S(1)}, bf16[128,1792]{1,0:T(8,128)(2,1)}, u32[]{:S(2)}) copy-start(bf16[128,1792]{1,0:T(8,128)(2,1)} %up_hbm.1) | copy-start | bytes 1376260
  2.0 0.9 %copy-start.2 = (bf16[1792,64]{0,1:T(8,128)(2,1)S(1)}, bf16[1792,64]{0,1:T(8,128)(2,1)}, u32[]{:S(2)}) copy-start(bf16[1792,64]{0,1:T(8,128)(2,1)} %param.5) | copy-start | bytes 688132

commit v2 on v0

v2 whole, which is shorter than its diff:
```python
import jax
import jax.numpy as jnp
from jax import lax
from jax.experimental import pallas as pl
from jax.experimental.pallas import tpu as pltpu
from jax.sharding import PartitionSpec as P

MESH = pl.DeviceIdType.MESH
X, Y, Z = 4, 8, 8
ROWS, COLS, HALF = 128, 64, 896


def kernel(
    gate_hbm, up_hbm, w_hbm, out_ref,
    gate, up, h_send, a_all, b_all, part, other, s_buf, r_buf, f_buf, fin,
    load_sem, wx_sem, ax_sem, x_sem, z_sem, c_sem, y_sem, f_sem,
):
    f, t = lax.axis_index("fsdp"), lax.axis_index("tp")
    x, q, z = (f // 2) % X, f % 2, f // (2 * X)
    y, c = (t // 2) * 2 + q, t % 2
    p = 1 - q
    sent = []

    def at(dx=0, dy=0, dz=0, core=c):
        to_x, to_y, to_z = (x + X + dx) % X, (y + Y + dy) % Y, (z + Z + dz) % Z
        return (to_z * 2 * X + to_x * 2 + to_y % 2, (to_y // 2) * 2 + core)

    mate = at(dy=1 - 2 * q)
    twin = at(core=1 - c)

    def send(src, dst, sems, device):
        copy = pltpu.make_async_remote_copy(
            src_ref=src, dst_ref=dst, send_sem=sems.at[0], recv_sem=sems.at[1],
            device_id=device, device_id_type=MESH,
        )
        copy.start()
        sent.append(copy)
        return copy

    mine = pl.ds(pl.multiple_of(q * HALF, 128), HALF)
    theirs = pl.ds(pl.multiple_of(p * HALF, 128), HALF)

    def a_at(x, q, start=0, size=ROWS):
        return a_all.at[q, pl.ds(pl.multiple_of(x * ROWS + start, 16), size)]

    def b_at(z, q, start=0, size=COLS):
        return b_all.at[pl.ds(pl.multiple_of((z * 2 + q) * COLS + start, 16), size)]

    loads = [
        pltpu.make_async_copy(w_hbm.at[:, mine], b_at(z, q), load_sem.at[0]),
        pltpu.make_async_copy(gate_hbm.at[:, theirs], gate.at[1], load_sem.at[1]),
        pltpu.make_async_copy(up_hbm.at[:, theirs], up.at[1], load_sem.at[2]),
        pltpu.make_async_copy(gate_hbm.at[:, mine], gate.at[0], load_sem.at[3]),
        pltpu.make_async_copy(up_hbm.at[:, mine], up.at[0], load_sem.at[4]),
    ]
    for load in loads:
        load.start()

    barrier = pltpu.get_barrier_semaphore()
    peers = [at(dx, dy) for dx in range(X) for dy in range(-2, 3) if (dx, dy) != (0, 0)]
    peers += [at(dz=dz) for dz in (-2, -1, 1, 2)] + [twin]
    for peer in peers:
        pl.semaphore_signal(barrier, inc=1, device_id=peer, device_id_type=MESH)
    pl.semaphore_wait(barrier, len(peers))

    part_w = COLS // 2
    w_swap = [
        send(
            w_hbm.at[pl.ds(i * part_w, part_w), theirs], b_at(z, q, i * part_w, part_w),
            wx_sem.at[i], mate,
        )
        for i in range(2)
    ]

    def z_hop(step, piece):
        who = q if piece < 2 else p
        hop, far = (2, 2) if step == 3 else (1, step)
        size = part_w // 2 if step == 3 else part_w
        start = (piece % 2) * part_w
        ahead = b_at((z + Z - far) % Z, who, start, size)
        behind = b_at((z + far) % Z, who, start + part_w - size, size)
        return [
            send(ahead, ahead, z_sem.at[0, step, piece], at(dz=hop)),
            send(behind, behind, z_sem.at[1, step, piece], at(dz=-hop)),
        ]

    def x_hop(piece):
        src = a_at(x, q if piece < 2 else p, (piece % 2) * 64, 64)
        return [send(src, src, x_sem.at[i, piece], at(dx=d)) for i, d in enumerate((1, 3, 2))]

    def landed(copies):
        for copy in copies:
            copy.wait_recv()

    def act(i):
        g = gate[i].astype(jnp.float32)
        return (g / (1.0 + jnp.exp(-g)) * up[i].astype(jnp.float32)).astype(jnp.bfloat16)

    zs, xs = {}, {}
    loads[0].wait()
    for i in (0, 1):
        zs[0, i] = z_hop(0, i)
    loads[1].wait()
    loads[2].wait()
    h_send[...] = act(1)
    a_swap = [
        send(h_send.at[pl.ds(i * 64, 64)], a_at(x, q, i * 64, 64), ax_sem.at[i], mate)
        for i in range(2)
    ]
    loads[3].wait()
    loads[4].wait()
    a_at(x, q)[...] = act(0)
    for i in (0, 1):
        xs[i] = x_hop(i)
    for i in (2, 3):
        w_swap[i - 2].wait_recv()
        zs[0, i] = z_hop(0, i)
    for i in (0, 1):
        landed(zs[0, i])
        zs[1, i] = z_hop(1, i)
    for i in (2, 3):
        a_swap[i - 2].wait_recv()
        xs[i] = x_hop(i)
    for i in (2, 3):
        landed(zs[0, i])
        zs[1, i] = z_hop(1, i)
    for pair in ((0, 1), (2, 3)):
        for i in pair:
            landed(zs[1, i])
            zs[3, i] = z_hop(3, i)
            zs[2, i] = z_hop(2, i)
    for i in range(4):
        landed(xs[i])
        landed(zs[2, i])
        landed(zs[3, i])

    def core_copy(to):
        return pltpu.make_async_remote_copy(
            src_ref=part.at[1 - c, to], dst_ref=other.at[to],
            send_sem=c_sem.at[0, to], recv_sem=c_sem.at[1, to],
            device_id=twin, device_id_type=MESH,
        )

    def product(i, carry):
        odd = i % 2
        to = (y + 4 + (1 - odd) * (i // 2) - odd * ((i + 1) // 2)) % Y
        b = b_all[pl.ds(pl.multiple_of((to // 2) * 256, 256), 256)]
        r = lax.dot_general(
            a_all[to % 2], b, (((1,), (1,)), ((), ())), preferred_element_type=jnp.float32
        )
        part[0, to] = r[:, :128]
        part[1, to] = r[:, 128:]
        core_copy(to).start()
        return carry

    lax.fori_loop(0, Y, product, 0)

    def own(to, start=0, size=X * ROWS):
        rows = pl.ds(start, size)
        return part[c, to, rows] + other[to, rows]

    half = 2 * ROWS

    def settle(offset):
        to = (y + Y + offset) % Y
        core_copy(to).wait_recv()
        return to

    to = settle(4)
    s_buf[0] = own(to).astype(jnp.bfloat16)
    far = [
        send(s_buf.at[0, pl.ds(i * half, half)], r_buf.at[0, pl.ds(i * half, half)], y_sem.at[i], at(dy=d))
        for i, d in enumerate((2, -2))
    ]
    near = {}
    for i, offset in ((1, 3), (2, -3)):
        to = settle(offset)
        s_buf[i] = own(to).astype(jnp.bfloat16)
        near[i] = send(s_buf.at[i], r_buf.at[i], y_sem.at[1 + i], at(dy=1 if offset > 0 else -1))

    lasts = []

    def final(offset):
        for k in (2, 1, 3, 0):
            if (k, offset) != (0, 0):
                i = (x + k) % X
                lasts.append(
                    send(f_buf.at[offset + 2, i], fin.at[offset + 2, x], f_sem.at[offset + 2, k], at(dx=k, dy=offset))
                )

    for offset in (1, -1):
        to = settle(offset)
        f_buf[offset + 2] = own(to).astype(jnp.bfloat16).reshape(X, ROWS, 128)
        final(offset)
    for i, offset in ((0, 2), (1, -2)):
        to = settle(offset)
        far[i].wait_recv()
        near[1 + i].wait_recv()
        total = own(to) + r_buf[1 + i].astype(jnp.float32)
        mid = r_buf[0, i * half : (i + 1) * half].astype(jnp.float32)
        with_far = (total[i * half : (i + 1) * half] + mid).astype(jnp.bfloat16)
        rest = total[(1 - i) * half : (2 - i) * half].astype(jnp.bfloat16)
        f_buf[offset + 2, 2 * i : 2 * i + 2] = with_far.reshape(2, ROWS, 128)
        f_buf[offset + 2, 2 - 2 * i : 4 - 2 * i] = rest.reshape(2, ROWS, 128)
        final(offset)
    to = settle(0)
    f_buf[2] = own(to).astype(jnp.bfloat16).reshape(X, ROWS, 128)
    final(0)
    fin[2, x] = f_buf[2, x]
    for copy in lasts:
        copy.wait_recv()
    for i in range(X):
        total = fin[0, i].astype(jnp.float32)
        for j in range(1, 5):
            total = total + fin[j, i].astype(jnp.float32)
        out_ref[:, i * 128 : (i + 1) * 128] = total.astype(jnp.bfloat16)
    for copy in sent:
        copy.wait_send()
    for i in range(Y):
        core_copy(i).wait_send()


def shards(gate_pre, up_pre, down_weight):
    dma = pltpu.SemaphoreType.DMA
    bf16, f32 = jnp.bfloat16, jnp.float32
    return pl.pallas_call(
        kernel,
        out_shape=jax.ShapeDtypeStruct((ROWS, 512), bf16),
        in_specs=[pl.BlockSpec(memory_space=pl.ANY)] * 3,
        out_specs=pl.BlockSpec(memory_space=pltpu.VMEM),
        scratch_shapes=[
            pltpu.VMEM((2, ROWS, HALF), bf16),
            pltpu.VMEM((2, ROWS, HALF), bf16),
            pltpu.VMEM((ROWS, HALF), bf16),
            pltpu.VMEM((2, X * ROWS, HALF), bf16),
            pltpu.VMEM((Z * 2 * COLS, HALF), bf16),
            pltpu.VMEM((2, Y, X * ROWS, 128), f32),
            pltpu.VMEM((Y, X * ROWS, 128), f32),
            pltpu.VMEM((3, X * ROWS, 128), bf16),
            pltpu.VMEM((3, X * ROWS, 128), bf16),
            pltpu.VMEM((5, X, ROWS, 128), bf16),
            pltpu.VMEM((5, X, ROWS, 128), bf16),
            dma((5,)),
            dma((2, 2)),
            dma((2, 2)),
            dma((3, 4, 2)),
            dma((2, 4, 4, 2)),
            dma((2, Y)),
            dma((4, 2)),
            dma((5, X, 2)),
        ],
        compiler_params=pltpu.CompilerParams(
            collective_id=0, has_side_effects=True, vmem_limit_bytes=55000 * 1024
        ),
        name="down_projection",
    )(gate_pre, up_pre, down_weight.T)


def solution(mesh):
    return jax.shard_map(
        shards,
        mesh=mesh,
        in_specs=(P("fsdp", "tp"), P("fsdp", "tp"), P("tp", "fsdp")),
        out_specs=P("fsdp", "tp"),
        check_vma=False,
    )
```

time: 456 us -> 58.9 us (0.13)
  the two profiles are of different devices: /device:TPU:1 before, /device:TPU:6 now
where the time goes in v2:
time: 58.9 us; the launch traced here: 58.8 us
  Pallas kernels  58.1 us (99%)
  local copies, waits for them, and re-layouts  0.66 us (1%)
    pallas_call x1, Pallas kernels, shards(): pl.pallas_call(kernel, out_shape=jax.ShapeDtypeStruct((ROWS, 512), bf16),...  58.1 us

profile of v2, /device:TPU:6, one launch (start us, length us, event | category | flops | bytes accessed | tf_op | source)
XLA Modules:
  0.0 58.8 jit_solution(11464678732946650605)
XLA Ops:
  0.0 58.1 %down_projection.1 = bf16[128,512]{1,0:T(8,128)(2,1)S(1)} custom-call(bf16[128,1792]{1,0:T(8,128)(2,1)} %gate_hbm.1, bf16[128,1792]{1,0:T(8,128)(2,1)} %up_hbm.1, bf16[64,1792]{1,0:T(8,128)(2,1)} %bitcast.1), custom_call_target="tpu_custom_call" | custom-call | tf_op jit(solution)/shard_map/down_projection/pallas_call | solution.py:226
  58.1 0.7 %copy.5 = bf16[128,512]{1,0:T(8,128)(2,1)} copy(bf16[128,512]{1,0:T(8,128)(2,1)S(1)} %down_projection.1) | data formatting | bytes 262144

commit v3 on v2

v3 whole, which is shorter than its diff:
```python
import jax
import jax.numpy as jnp
from jax import lax
from jax.experimental import pallas as pl
from jax.experimental.pallas import tpu as pltpu
from jax.sharding import PartitionSpec as P

MESH = pl.DeviceIdType.MESH
X, Y, Z = 4, 8, 8
ROWS, COLS, HALF = 128, 64, 896


def kernel(
    gate_hbm, up_hbm, w_hbm, out_ref,
    gate, up, h_send, a_all, b_all, part, other, s_buf, r_buf, f_buf, fin,
    load_sem, wx_sem, ax_sem, x_sem, z_sem, c_sem, y_sem, f_sem, relay,
):
    rem, div = lax.rem, lax.div
    f, t = lax.axis_index("fsdp"), lax.axis_index("tp")
    x, q, z = rem(div(f, 2), X), rem(f, 2), div(f, 2 * X)
    y, c = div(t, 2) * 2 + q, rem(t, 2)
    p = 1 - q
    sent = []

    def at(dx=0, dy=0, dz=0, core=c):
        to_x = x if isinstance(dx, int) and dx == 0 else rem(x + (X + dx), X)
        to_y = y if isinstance(dy, int) and dy == 0 else rem(y + (Y + dy), Y)
        to_z = z if isinstance(dz, int) and dz == 0 else rem(z + (Z + dz), Z)
        return (to_z * (2 * X) + to_x * 2 + rem(to_y, 2), div(to_y, 2) * 2 + core)

    mate = at(dy=1 - 2 * q)
    twin = at(core=1 - c)

    def copy_to(src, dst, sems, device):
        return pltpu.make_async_remote_copy(
            src_ref=src, dst_ref=dst, send_sem=sems.at[0], recv_sem=sems.at[1],
            device_id=device, device_id_type=MESH,
        )

    def send(*args):
        copy = copy_to(*args)
        copy.start()
        sent.append(copy)
        return copy

    def each(n, body, start=0):
        def step(i, carry):
            body(i)
            return carry

        lax.fori_loop(start, n, step, 0)

    mine = pl.ds(pl.multiple_of(q * HALF, 128), HALF)
    theirs = pl.ds(pl.multiple_of(p * HALF, 128), HALF)

    def a_at(x, q, start=0, size=ROWS):
        return a_all.at[q, pl.ds(pl.multiple_of(x * ROWS + start, 16), size)]

    def b_at(z, q, start=0, size=COLS):
        return b_all.at[pl.ds(pl.multiple_of((z * 2 + q) * COLS + start, 16), size)]

    loads = [
        pltpu.make_async_copy(w_hbm.at[:, mine], b_at(z, q), load_sem.at[0]),
        pltpu.make_async_copy(gate_hbm.at[:, theirs], gate.at[1], load_sem.at[1]),
        pltpu.make_async_copy(up_hbm.at[:, theirs], up.at[1], load_sem.at[2]),
        pltpu.make_async_copy(gate_hbm.at[:, mine], gate.at[0], load_sem.at[3]),
        pltpu.make_async_copy(up_hbm.at[:, mine], up.at[0], load_sem.at[4]),
    ]
    for load in loads:
        load.start()

    barrier = pltpu.get_barrier_semaphore()

    def greet(device):
        pl.semaphore_signal(barrier, inc=1, device_id=device, device_id_type=MESH)

    up_z, down_z = at(dz=1), at(dz=-1)
    greet(up_z)
    greet(down_z)
    greet(at(dy=1))
    greet(at(dy=-1))
    greet(at(1))
    greet(at(3))
    greet(twin)
    def act(i, dst):
        def rows(r):
            at_rows = pl.ds(pl.multiple_of(r * 16, 16), 16)
            g = gate[i, at_rows].astype(jnp.float32)
            h = g / (1.0 + jnp.exp(-g)) * up[i, at_rows].astype(jnp.float32)
            dst[at_rows] = h.astype(jnp.bfloat16)

        each(ROWS // 16, rows)

    loads[1].wait()
    loads[2].wait()
    act(1, h_send)
    loads[3].wait()
    loads[4].wait()
    act(0, a_at(x, q))
    pl.semaphore_wait(barrier, 7)
    for dy in (1, -1):
        pl.semaphore_signal(relay, inc=1, device_id=at(dy=dy), device_id_type=MESH)

    cut = COLS // 2
    w_swap = [
        send(w_hbm.at[pl.ds(i * cut, cut), theirs], b_at(z, q, i * cut, cut), wx_sem.at[i], mate)
        for i in range(2)
    ]

    def z_hop(step, piece):
        who = p if piece > 1 else q
        far, size = (2, cut // 2) if step == 3 else (step, cut)
        start = piece % 2 * cut
        ahead = b_at(rem(z + (Z - far), Z), who, start, size)
        behind = b_at(rem(z + far, Z), who, start + cut - size, size)
        return [
            send(ahead, ahead, z_sem.at[0, step, piece], at(dz=2) if step == 3 else up_z),
            send(behind, behind, z_sem.at[1, step, piece], at(dz=-2) if step == 3 else down_z),
        ]

    right, left = at(1), at(3)

    def x_hop(piece):
        src = a_at(x, p if piece > 1 else q, piece % 2 * 64, 64)
        return [send(src, src, x_sem.at[i, piece], d) for i, d in enumerate((right, left))]

    def x_on(piece):
        i = piece % 2
        src = a_at(rem(x + (3 if i == 0 else 1), X), p if piece > 1 else q, i * 64, 64)
        return [send(src, src, x_sem.at[2, piece], right if i == 0 else left)]

    def landed(copies):
        for copy in copies:
            copy.wait_recv()

    zs, xs, xo = {}, {}, {}
    loads[0].wait()
    for i in (0, 1):
        zs[0, i] = z_hop(0, i)
    a_swap = [
        send(h_send.at[pl.ds(i * 64, 64)], a_at(x, q, i * 64, 64), ax_sem.at[i], mate) for i in range(2)
    ]
    for i in (0, 1):
        xs[i] = x_hop(i)
    for i in (2, 3):
        w_swap[i - 2].wait_recv()
        zs[0, i] = z_hop(0, i)
    for i in (0, 1):
        landed(zs[0, i])
        zs[1, i] = z_hop(1, i)
    pl.semaphore_wait(relay, 2)
    for i in (2, 3):
        a_swap[i - 2].wait_recv()
        xs[i] = x_hop(i)
    for i in (0, 1):
        landed(xs[i])
        xo[i] = x_on(i)
    for i in (2, 3):
        landed(zs[0, i])
        zs[1, i] = z_hop(1, i)
    for i in (0, 1):
        landed(zs[1, i])
        zs[3, i] = z_hop(3, i)
        zs[2, i] = z_hop(2, i)
    for i in (2, 3):
        landed(xs[i])
        xo[i] = x_on(i)
    for i in (2, 3):
        landed(zs[1, i])
        zs[3, i] = z_hop(3, i)
        zs[2, i] = z_hop(2, i)
    near_z = [copy for i in range(4) for copy in zs[2, i]]
    far_z = [copy for i in range(4) for copy in zs[3, i]]
    for i in range(4):
        landed(xo[i])

    def core_copy(to):
        return copy_to(part.at[1 - c, to], other.at[to], c_sem.at[to], twin)

    def product(i):
        pl.when(i == 5)(lambda: landed(near_z))
        pl.when(i == 7)(lambda: landed(far_z))
        odd = rem(i, 2)
        zz = rem(z + odd * div(i + 1, 2) + (1 - odd) * (Z - div(i, 2)), Z)
        owner, to = rem(zz, 2), div(zz, 2) * 2
        b = b_all[pl.ds(pl.multiple_of(zz * 128, 128), 128)]

        def block(j):
            part[owner, to + j] = lax.dot_general(
                a_all[j], b, (((1,), (1,)), ((), ())), preferred_element_type=jnp.float32
            )

        each(2, block)

        @pl.when(owner != c)
        def _():
            core_copy(to).start()
            core_copy(to + 1).start()

    half = 2 * ROWS

    def settle(offset):
        to = rem(y + Y + offset, Y)
        core_copy(to).wait_recv()
        return to

    def pack(to, dst, start=0, stop=X, extra=()):
        def chunk(k):
            rows = pl.ds(pl.multiple_of(k * ROWS, ROWS), ROWS)
            v = part[c, to, rows] + other[to, rows]
            for e in extra:
                v = v + e[rows].astype(jnp.float32)
            dst[rows] = v.astype(jnp.bfloat16)

        each(stop, chunk, start)

    def far(i):
        rows = pl.ds(i * half, half)
        return copy_to(s_buf.at[0, rows], r_buf.at[0, rows], y_sem.at[i], at(dy=-2 if i else 2))

    def near(i):
        return copy_to(s_buf.at[1 + i], r_buf.at[1 + i], y_sem.at[2 + i], at(dy=-1 if i else 1))

    def when_due(offset, batch, body):
        to = rem(y + Y + offset, Y)
        dz = rem(div(to, 2) * 2 + c + (Z + 2) - z, Z)
        late = (dz > 4).astype(jnp.int32)

        @pl.when(late == batch)
        def _():
            body(to)

    def last(offset, k):
        rows = pl.ds(pl.multiple_of(rem(x + k, X) * ROWS, ROWS), ROWS)
        return copy_to(f_buf.at[offset + 2, rows], fin.at[offset + 2, x], f_sem.at[offset + 2, k], at(k, offset))

    def final(offset):
        each(X, lambda k: last(offset, k).start(), 1 if isinstance(offset, int) and offset == 0 else 0)

    def send_far(to):
        settle(4)
        pack(to, s_buf.at[0])
        far(0).start()
        far(1).start()

    def send_near(i, offset):
        def body(to):
            settle(offset)
            pack(to, s_buf.at[1 + i])
            near(i).start()

        return body

    def send_own(offset):
        def body(to):
            settle(offset)
            pack(to, f_buf.at[offset + 2])
            final(offset)

        return body

    def send_sum(i, offset):
        def body(to):
            settle(offset)
            far(i).wait_recv()
            near(i).wait_recv()
            pack(to, f_buf.at[offset + 2], 2 * i, 2 * i + 2, (r_buf.at[0], r_buf.at[1 + i]))
            pack(to, f_buf.at[offset + 2], 2 - 2 * i, 4 - 2 * i, (r_buf.at[1 + i],))
            final(offset)

        return body

    def batch(b):
        each(5 + 3 * b, product, 5 * b)
        when_due(4, b, send_far)
        when_due(3, b, send_near(0, 3))
        when_due(-3, b, send_near(1, -3))
        for offset in (1, -1, 0):
            when_due(offset, b, send_own(offset))

    each(2, batch)

    def sums(b):
        when_due(2, b, send_sum(0, 2))
        when_due(-2, b, send_sum(1, -2))

    each(2, sums)
    fin[2, x] = f_buf[2, pl.ds(pl.multiple_of(x * ROWS, ROWS), ROWS)]
    for offset in (0, 1, -1, 2, -2):
        each(X, lambda k: last(offset, k).wait_recv(), 0 if offset else 1)

    def add_up(i):
        total = fin[0, i].astype(jnp.float32)
        for j in range(1, 5):
            total = total + fin[j, i].astype(jnp.float32)
        out_ref[:, pl.ds(pl.multiple_of(i * 128, 128), 128)] = total.astype(jnp.bfloat16)

    each(X, add_up)
    for copy in sent + [far(0), far(1), near(0), near(1)]:
        copy.wait_send()
    each(Y, lambda i: core_copy(i).wait_send())
    for offset in (0, 1, -1, 2, -2):
        each(X, lambda k: last(offset, k).wait_send(), 0 if offset else 1)


def shards(gate_pre, up_pre, down_weight):
    dma = pltpu.SemaphoreType.DMA
    bf16, f32 = jnp.bfloat16, jnp.float32
    return pl.pallas_call(
        kernel,
        out_shape=jax.ShapeDtypeStruct((ROWS, 512), bf16),
        in_specs=[pl.BlockSpec(memory_space=pl.ANY)] * 3,
        out_specs=pl.BlockSpec(memory_space=pltpu.VMEM),
        scratch_shapes=[
            pltpu.VMEM((2, ROWS, HALF), bf16),
            pltpu.VMEM((2, ROWS, HALF), bf16),
            pltpu.VMEM((ROWS, HALF), bf16),
            pltpu.VMEM((2, X * ROWS, HALF), bf16),
            pltpu.VMEM((Z * 2 * COLS, HALF), bf16),
            pltpu.VMEM((2, Y, X * ROWS, 128), f32),
            pltpu.VMEM((Y, X * ROWS, 128), f32),
            pltpu.VMEM((3, X * ROWS, 128), bf16),
            pltpu.VMEM((3, X * ROWS, 128), bf16),
            pltpu.VMEM((5, X * ROWS, 128), bf16),
            pltpu.VMEM((5, X, ROWS, 128), bf16),
            dma((5,)),
            dma((2, 2)),
            dma((2, 2)),
            dma((3, 4, 2)),
            dma((2, 4, 4, 2)),
            dma((Y, 2)),
            dma((4, 2)),
            dma((5, X, 2)),
            pltpu.SemaphoreType.REGULAR,
        ],
        compiler_params=pltpu.CompilerParams(
            collective_id=0, has_side_effects=True, vmem_limit_bytes=55000 * 1024
        ),
        name="down_projection",
    )(gate_pre, up_pre, down_weight.T)


def solution(mesh):
    return jax.shard_map(
        shards,
        mesh=mesh,
        in_specs=(P("fsdp", "tp"), P("fsdp", "tp"), P("tp", "fsdp")),
        out_specs=P("fsdp", "tp"),
        check_vma=False,
    )
```

time: 58.9 us -> 56.3 us (0.956)
  the two profiles are of different devices: /device:TPU:6 before, /device:TPU:1 now
where the time goes in v3:
time: 56.3 us; the launch traced here: 55.8 us
  Pallas kernels  55.1 us (98%)
  local copies, waits for them, and re-layouts  0.66 us (1%)
    pallas_call x1, Pallas kernels, shards(): pl.pallas_call(kernel, out_shape=jax.ShapeDtypeStruct((ROWS, 512), bf16),...  55.1 us

profile of v3, /device:TPU:1, one launch (start us, length us, event | category | flops | bytes accessed | tf_op | source)
XLA Modules:
  0.0 55.8 jit_solution(14533448447596587205)
XLA Ops:
  0.0 55.1 %down_projection.1 = bf16[128,512]{1,0:T(8,128)(2,1)S(1)} custom-call(bf16[128,1792]{1,0:T(8,128)(2,1)} %gate_hbm.1, bf16[128,1792]{1,0:T(8,128)(2,1)} %up_hbm.1, bf16[64,1792]{1,0:T(8,128)(2,1)} %bitcast.1), custom_call_target="tpu_custom_call" | custom-call | tf_op jit(solution)/shard_map/down_projection/pallas_call | solution.py:309
  55.1 0.7 %copy.5 = bf16[128,512]{1,0:T(8,128)(2,1)} copy(bf16[128,512]{1,0:T(8,128)(2,1)S(1)} %down_projection.1) | data formatting | bytes 262144

commit v4 on v3

--- a/solution.py
+++ b/solution.py
@@ -91,12 +91,6 @@
 
         each(ROWS // 16, rows)
 
-    loads[1].wait()
-    loads[2].wait()
-    act(1, h_send)
-    loads[3].wait()
-    loads[4].wait()
-    act(0, a_at(x, q))
     pl.semaphore_wait(barrier, 7)
     for dy in (1, -1):
         pl.semaphore_signal(relay, inc=1, device_id=at(dy=dy), device_id_type=MESH)
@@ -137,9 +131,15 @@
     loads[0].wait()
     for i in (0, 1):
         zs[0, i] = z_hop(0, i)
+    loads[1].wait()
+    loads[2].wait()
+    act(1, h_send)
     a_swap = [
         send(h_send.at[pl.ds(i * 64, 64)], a_at(x, q, i * 64, 64), ax_sem.at[i], mate) for i in range(2)
     ]
+    loads[3].wait()
+    loads[4].wait()
+    act(0, a_at(x, q))
     for i in (0, 1):
         xs[i] = x_hop(i)
     for i in (2, 3):
@@ -152,23 +152,23 @@
     for i in (2, 3):
         a_swap[i - 2].wait_recv()
         xs[i] = x_hop(i)
+    for i in (2, 3):
+        landed(zs[0, i])
+        zs[1, i] = z_hop(1, i)
     for i in (0, 1):
         landed(xs[i])
         xo[i] = x_on(i)
-    for i in (2, 3):
-        landed(zs[0, i])
-        zs[1, i] = z_hop(1, i)
     for i in (0, 1):
         landed(zs[1, i])
+        zs[2, i] = z_hop(2, i)
         zs[3, i] = z_hop(3, i)
-        zs[2, i] = z_hop(2, i)
     for i in (2, 3):
         landed(xs[i])
         xo[i] = x_on(i)
     for i in (2, 3):
         landed(zs[1, i])
+        zs[2, i] = z_hop(2, i)
         zs[3, i] = z_hop(3, i)
-        zs[2, i] = z_hop(2, i)
     near_z = [copy for i in range(4) for copy in zs[2, i]]
     far_z = [copy for i in range(4) for copy in zs[3, i]]
     for i in range(4):
@@ -235,7 +235,12 @@
         return copy_to(f_buf.at[offset + 2, rows], fin.at[offset + 2, x], f_sem.at[offset + 2, k], at(k, offset))
 
     def final(offset):
-        each(X, lambda k: last(offset, k).start(), 1 if isinstance(offset, int) and offset == 0 else 0)
+        if offset:
+            last(offset, 2).start()
+        for k in (1, 3) if offset else (2, 1, 3):
+            last(offset, k).start()
+        if offset:
+            last(offset, 0).start()
 
     def send_far(to):
         settle(4)
@@ -286,6 +291,11 @@
 
     each(2, sums)
     fin[2, x] = f_buf[2, pl.ds(pl.multiple_of(x * ROWS, ROWS), ROWS)]
+    for copy in sent + [far(0), far(1), near(0), near(1)]:
+        copy.wait_send()
+    each(Y, lambda i: core_copy(i).wait_send())
+    for offset in (0, 1, -1, 2, -2):
+        each(X, lambda k: last(offset, k).wait_send(), 0 if offset else 1)
     for offset in (0, 1, -1, 2, -2):
         each(X, lambda k: last(offset, k).wait_recv(), 0 if offset else 1)
 
@@ -296,11 +306,6 @@
         out_ref[:, pl.ds(pl.multiple_of(i * 128, 128), 128)] = total.astype(jnp.bfloat16)
 
     each(X, add_up)
-    for copy in sent + [far(0), far(1), near(0), near(1)]:
-        copy.wait_send()
-    each(Y, lambda i: core_copy(i).wait_send())
-    for offset in (0, 1, -1, 2, -2):
-        each(X, lambda k: last(offset, k).wait_send(), 0 if offset else 1)
 
 
 def shards(gate_pre, up_pre, down_weight):

time: 56.3 us -> 55.9 us (level)
  Pallas kernels: 55.1 us -> 54.4 us
    pallas_call x1, Pallas kernels: 55.1 us -> 54.4 us  [shards(): pl.pallas_call(kernel, out_shape=jax.ShapeDtypeStruct((ROWS, 512), bf16),...]
where the time goes in v4:
time: 55.9 us; the launch traced here: 55.1 us
  Pallas kernels  54.4 us (97%)
  local copies, waits for them, and re-layouts  0.66 us (1%)
    pallas_call x1, Pallas kernels, shards(): pl.pallas_call(kernel, out_shape=jax.ShapeDtypeStruct((ROWS, 512), bf16),...  54.4 us

profile of v4, /device:TPU:1, one launch (start us, length us, event | category | flops | bytes accessed | tf_op | source)
XLA Modules:
  0.0 55.1 jit_solution(6943850635928705164)
XLA Ops:
  0.0 54.4 %down_projection.1 = bf16[128,512]{1,0:T(8,128)(2,1)S(1)} custom-call(bf16[128,1792]{1,0:T(8,128)(2,1)} %gate_hbm.1, bf16[128,1792]{1,0:T(8,128)(2,1)} %up_hbm.1, bf16[64,1792]{1,0:T(8,128)(2,1)} %bitcast.1), custom_call_target="tpu_custom_call" | custom-call | tf_op jit(solution)/shard_map/down_projection/pallas_call | solution.py:314
  54.4 0.7 %copy.5 = bf16[128,512]{1,0:T(8,128)(2,1)} copy(bf16[128,512]{1,0:T(8,128)(2,1)S(1)} %down_projection.1) | data formatting | bytes 262144

commit v5 on v4

--- a/solution.py
+++ b/solution.py
@@ -114,14 +114,18 @@
 
     right, left = at(1), at(3)
 
+    def x_piece(piece):
+        return (piece * 64, 64, piece) if piece < 2 else ((piece - 2) * 32, 32, (piece - 2) // 2)
+
     def x_hop(piece):
-        src = a_at(x, p if piece > 1 else q, piece % 2 * 64, 64)
+        start, size, _ = x_piece(piece)
+        src = a_at(x, p if piece > 1 else q, start, size)
         return [send(src, src, x_sem.at[i, piece], d) for i, d in enumerate((right, left))]
 
     def x_on(piece):
-        i = piece % 2
-        src = a_at(rem(x + (3 if i == 0 else 1), X), p if piece > 1 else q, i * 64, 64)
-        return [send(src, src, x_sem.at[2, piece], right if i == 0 else left)]
+        start, size, way = x_piece(piece)
+        src = a_at(rem(x + (1 if way else 3), X), p if piece > 1 else q, start, size)
+        return [send(src, src, x_sem.at[2, piece], left if way else right)]
 
     def landed(copies):
         for copy in copies:
@@ -135,7 +139,7 @@
     loads[2].wait()
     act(1, h_send)
     a_swap = [
-        send(h_send.at[pl.ds(i * 64, 64)], a_at(x, q, i * 64, 64), ax_sem.at[i], mate) for i in range(2)
+        send(h_send.at[pl.ds(i * 32, 32)], a_at(x, q, i * 32, 32), ax_sem.at[i], mate) for i in range(4)
     ]
     loads[3].wait()
     loads[4].wait()
@@ -149,7 +153,7 @@
         landed(zs[0, i])
         zs[1, i] = z_hop(1, i)
     pl.semaphore_wait(relay, 2)
-    for i in (2, 3):
+    for i in range(2, 6):
         a_swap[i - 2].wait_recv()
         xs[i] = x_hop(i)
     for i in (2, 3):
@@ -162,7 +166,7 @@
         landed(zs[1, i])
         zs[2, i] = z_hop(2, i)
         zs[3, i] = z_hop(3, i)
-    for i in (2, 3):
+    for i in range(2, 6):
         landed(xs[i])
         xo[i] = x_on(i)
     for i in (2, 3):
@@ -171,7 +175,7 @@
         zs[3, i] = z_hop(3, i)
     near_z = [copy for i in range(4) for copy in zs[2, i]]
     far_z = [copy for i in range(4) for copy in zs[3, i]]
-    for i in range(4):
+    for i in range(6):
         landed(xo[i])
 
     def core_copy(to):
@@ -330,8 +334,8 @@
             pltpu.VMEM((5, X, ROWS, 128), bf16),
             dma((5,)),
             dma((2, 2)),
-            dma((2, 2)),
-            dma((3, 4, 2)),
+            dma((4, 2)),
+            dma((3, 6, 2)),
             dma((2, 4, 4, 2)),
             dma((Y, 2)),
             dma((4, 2)),

time: 55.9 us -> 54.5 us (0.975)
  Pallas kernels: 54.4 us -> 53 us
    pallas_call x1, Pallas kernels: 54.4 us -> 53 us  [shards(): pl.pallas_call(kernel, out_shape=jax.ShapeDtypeStruct((ROWS, 512), bf16),...]
where the time goes in v5:
time: 54.5 us; the launch traced here: 53.6 us
  Pallas kernels  53 us (97%)
  local copies, waits for them, and re-layouts  0.66 us (1%)
    pallas_call x1, Pallas kernels, shards(): pl.pallas_call(kernel, out_shape=jax.ShapeDtypeStruct((ROWS, 512), bf16),...  53 us

profile of v5, /device:TPU:1, one launch (start us, length us, event | category | flops | bytes accessed | tf_op | source)
XLA Modules:
  0.0 53.6 jit_solution(7682921917667791741)
XLA Ops:
  0.0 53.0 %down_projection.1 = bf16[128,512]{1,0:T(8,128)(2,1)S(1)} custom-call(bf16[128,1792]{1,0:T(8,128)(2,1)} %gate_hbm.1, bf16[128,1792]{1,0:T(8,128)(2,1)} %up_hbm.1, bf16[64,1792]{1,0:T(8,128)(2,1)} %bitcast.1), custom_call_target="tpu_custom_call" | custom-call | tf_op jit(solution)/shard_map/down_projection/pallas_call | solution.py:318
  53.0 0.7 %copy.5 = bf16[128,512]{1,0:T(8,128)(2,1)} copy(bf16[128,512]{1,0:T(8,128)(2,1)S(1)} %down_projection.1) | data formatting | bytes 262144
